TPU v7x, 32 devices: a whole 2x2x4 slice. The times are simulated.
32 devices in a mesh: dp: 16 (over z, y, core), seq: 2 (over x).
Axes of the slice: x: 2, y: 2, z: 4, core: 2. Of those that a mesh axis runs over, the one named last changes fastest.
Arguments:
- pre_act: bfloat16 [16, 512, 768], P('dp', 'seq'), may hold values from -6 to 6
- trunk_grad: bfloat16 [16, 256, 768], P('dp', None, 'seq'), may hold values from -6 to 6
- conv_weight: bfloat16 [5, 768, 768], P(None, 'dp'), may hold values from -0.09375 to 0.09375
- pair_weight: bfloat16 [768, 768], replicated, may hold values from -0.21875 to 0.21875
- donor_slots: int32 [16, 2, 2, 128], P('dp', 'seq'), may hold values from 0 to 255
- accept_slots: int32 [16, 2, 2, 128], P('dp', 'seq'), may hold values from 0 to 255
- junction_grad: float32 [16, 2, 2, 128], P('dp', 'seq'), may hold values from -6 to 6
- pair_counts: int32 [16, 2, 2], P('dp'), may hold values from 0 to 128, as said below
Outputs:
- input_grad: bfloat16 [16, 512, 768], P('dp', 'seq')
- pair_grad: float32 [768, 768], replicated
Inputs may be any that keep to these rules, and one draw needn't show every extreme that they name: pair_counts is at most 128; in every sample some acceptor slab has 128 live slots from every donor slab.
All inputs are finite; a program needn't handle non-finite values.
Results may differ from a plain program's by a relative error of at most 0.0061.
Values may be sent and summed in bfloat16 or wider, within the bound.
A program may use at most 64 MiB of HBM per device.

v0:
```python
import math

import jax
import jax.numpy as jnp
from jax import lax
from jax.sharding import PartitionSpec as P


def with_halo(x, sides, width):
    for axis, dim in sides:
        size, length = (lax.axis_size(axis), x.shape[dim])
        up = [(i, (i + 1) % size) for i in range(size - 1)]
        down = [(j, i) for i, j in up]
        last = lax.slice_in_dim(x, length - width, length, axis=dim)
        first = lax.slice_in_dim(x, 0, width, axis=dim)
        before = lax.ppermute(last, axis, up)
        after = lax.ppermute(first, axis, down)
        x = jnp.concatenate([before, x, after], axis=dim)
    return x


def gelu_parts(values):
    normal_cdf = 0.5 * (1.0 + jax.scipy.special.erf(values / math.sqrt(2.0)))
    density = jnp.exp(-0.5 * values * values) / math.sqrt(2.0 * math.pi)
    return (values * normal_cdf, normal_cdf + values * density)


def per_device(
    pre_act,
    trunk_grad,
    conv_weight,
    pair_weight,
    donor_slots,
    accept_slots,
    junction_grad,
    pair_counts,
):
    seq_count = lax.axis_size("seq")
    my_slab = lax.axis_index("seq")
    slab_len = pre_act.shape[1]
    channels = pre_act.shape[2]
    slot_count = donor_slots.shape[3]
    kernel = conv_weight.shape[0]
    half = kernel // 2
    act_f, slope = gelu_parts(pre_act[0].astype(jnp.float32))
    act = act_f.astype(jnp.bfloat16)
    arrived = lax.all_to_all(trunk_grad, "seq", split_axis=1, concat_axis=2, tiled=True)
    pooled = jnp.repeat(arrived[0].astype(jnp.float32) * 0.5, 2, axis=0)
    send_index = donor_slots[0, 0].reshape(-1)
    outgoing = act[send_index].reshape(seq_count, slot_count, channels)
    incoming = lax.all_to_all(outgoing, "seq", split_axis=0, concat_axis=0, tiled=True)
    donor_rows = incoming.reshape(-1, channels)
    accept_index = accept_slots[0, 0].reshape(-1)
    counts_in = lax.dynamic_index_in_dim(pair_counts[0], my_slab, axis=1, keepdims=False)
    live = jnp.arange(slot_count, dtype=jnp.int32)[None, :] < counts_in[:, None]
    slot_w = jnp.where(live, junction_grad[0, 0], 0.0).reshape(-1)
    accept_rows = act[accept_index]
    weighted = (slot_w[:, None] * accept_rows.astype(jnp.float32)).astype(jnp.bfloat16)
    accept_term = (
        jnp.dot(donor_rows, pair_weight, preferred_element_type=jnp.float32) * slot_w[:, None]
    )
    donor_term = lax.dot_general(
        weighted, pair_weight, (((1,), (1,)), ((), ())), preferred_element_type=jnp.float32
    ).astype(jnp.bfloat16)
    pair_part = lax.dot_general(
        donor_rows, weighted, (((0,), (0,)), ((), ())), preferred_element_type=jnp.float32
    )
    returned = lax.all_to_all(
        donor_term.reshape(seq_count, slot_count, channels),
        "seq",
        split_axis=0,
        concat_axis=0,
        tiled=True,
    )
    act_grad = (
        pooled.at[accept_index]
        .add(accept_term)
        .at[send_index]
        .add(returned.reshape(-1, channels).astype(jnp.float32))
    )
    conv_grad = (act_grad * slope).astype(jnp.bfloat16)
    padded = with_halo(conv_grad[None], (("seq", 1),), half)[0]
    piece = lax.all_gather(conv_weight, "dp", axis=1, tiled=True)
    total = jnp.zeros((slab_len, piece.shape[1]), jnp.float32)
    for tap in range(kernel):
        window = padded[2 * half - tap : 2 * half - tap + slab_len]
        total = total + lax.dot_general(
            window, piece[tap], (((1,), (1,)), ((), ())), preferred_element_type=jnp.float32
        )
    input_grad = total.astype(jnp.bfloat16)
    pair_sum = lax.psum(pair_part, ("dp", "seq"))
    scale = 1.0 / math.sqrt(lax.axis_size("dp") * seq_count * seq_count * slot_count)
    return (input_grad[None], pair_sum * scale)


def solution(mesh):
    in_specs = (
        P("dp", "seq", None),
        P("dp", None, "seq"),
        P(None, "dp", None),
        P(),
        P("dp", "seq", None, None),
        P("dp", "seq", None, None),
        P("dp", "seq", None, None),
        P("dp", None, None),
    )
    out_specs = (P("dp", "seq", None), P())
    return jax.shard_map(
        per_device, mesh=mesh, in_specs=in_specs, out_specs=out_specs, check_vma=False
    )
```

profile of v0, /device:TPU:1, one launch (start us, length us, event | category | flops | bytes accessed | tf_op | source)
XLA Modules:
  0.0 198.5 jit_solution(1862598864620470224)
XLA Ops:
  8.0 0.0 copy-start
  8.0 1.3 fusion.6
  9.3 0.0 copy-start.4
  9.3 0.7 compare_select_fusion
  10.0 1.9 gather_fusion
  11.9 0.0 copy-start.5
  11.9 0.0 copy-start.6
  11.9 3.6 %all-to-all-start.1 = ((bf16[2,128,768]{2,1,0:T(8,128)(2,1)}), bf16[2,128,768]{2,1,0:T(8,128)(2,1)S(1)}, u32[]{:S(2)}, u32[]{:S(2)}) async-start(bf16[2,128,768]{2,1,0:T(8,128)(2,1)} %bitcast.9), calls=%async_computation.1 | async-start | bytes 786432 | tf_op jit(solution)/shard_map/all_to_all | solution.py:51
  15.5 0.0 all-reduce.2.cloned.1.call-start
  15.6 0.0 copy-done.4
  15.6 1.2 gather_fusion.1
  16.8 0.0 copy-done.5
  16.8 0.2 dynamic-slice_reduce_fusion
  17.0 0.0 copy-done.6
  17.0 0.1 bitcast_select_fusion
  17.1 5.3 %all-to-all-done.1 = bf16[2,128,768]{2,1,0:T(8,128)(2,1)S(1)} async-done(((bf16[2,128,768]{2,1,0:T(8,128)(2,1)}), bf16[2,128,768]{2,1,0:T(8,128)(2,1)S(1)}, u32[]{:S(2)}, u32[]{:S(2)}) %all-to-all-start.1) | async-done | bytes 393248 | tf_op jit(solution)/shard_map/all_to_all | solution.py:51
  22.4 0.0 copy-start.3
  22.4 2.0 fusion.26
  24.4 0.0 all-reduce.2.cloned.1.call-update
  24.4 0.0 all-gather.2.cloned.1.call-start
  24.5 0.5 all-gather.2.cloned.1.call-update
  25.0 0.0 copy-done.3
  25.0 0.3 copy.19
  25.3 0.5 broadcast.65
  25.8 1.8 reduce.2
  27.6 0.7 reshape.152
  28.4 3.4 %all-to-all-start = ((bf16[2,2,24576]{2,1,0:T(2,128)(2,1)}), bf16[2,2,24576]{2,1,0:T(2,128)(2,1)S(1)}, u32[]{:S(2)}, u32[]{:S(2)}) async-start(bf16[2,2,24576]{2,1,0:T(2,128)(2,1)} %reshape.152), calls=%async_computation | async-start | bytes 393216 | tf_op jit(solution)/shard_map/all_to_all | solution.py:47
  31.8 0.0 copy-done
  31.8 1.3 convolution_convert_fusion
  33.1 2.7 %all-to-all-done = bf16[2,2,24576]{2,1,0:T(2,128)(2,1)S(1)} async-done(((bf16[2,2,24576]{2,1,0:T(2,128)(2,1)}), bf16[2,2,24576]{2,1,0:T(2,128)(2,1)S(1)}, u32[]{:S(2)}, u32[]{:S(2)}) %all-to-all-start) | async-done | bytes 196640 | tf_op jit(solution)/shard_map/all_to_all | solution.py:47
  35.8 4.2 %all-to-all-start.2 = ((bf16[2,128,768]{2,1,0:T(8,128)(2,1)}), bf16[2,128,768]{2,1,0:T(8,128)(2,1)}, u32[]{:S(2)}, u32[]{:S(2)}) async-start(bf16[2,128,768]{2,1,0:T(8,128)(2,1)} %bitcast.13), calls=%async_computation.2 | async-start | bytes 786432 | tf_op jit(solution)/shard_map/all_to_all | solution.py:68
  39.9 0.2 reshape.153
  40.2 0.2 copy.15
  40.4 0.2 copy.16
  40.5 0.3 broadcast_in_dim.10
  40.8 0.5 reshape.111
  41.4 0.5 convolution_multiply_fusion
  41.9 0.0 copy-start.1
  41.9 2.5 %scatter_fusion = f32[256,768]{1,0:T(8,128)S(1)} fusion(f32[256,768]{1,0:T(8,128)S(1)} %reshape.111, s32[256]{0:T(256)S(1)} %bitcast.77, f32[256,768]{1,0:T(8,128)S(1)} %convolution_multiply_fusion), kind=kCustom, calls=%fused_computation.2 | custom fusion | flops 196608 | bytes 2360320 | tf_op jit(solution)/shard_map/scatter-add | solution.py:77
  44.4 0.8 all-to-all-done.2
  45.2 3.0 %scatter_custom_fusion.1 = f32[256,768]{1,0:T(8,128)S(1)} fusion(f32[256,768]{1,0:T(8,128)S(1)} %scatter_fusion, s32[256]{0:T(256)S(1)} %bitcast.79, bf16[256,768]{1,0:T(8,128)(2,1)} %bitcast.27), kind=kCustom, calls=%fused_computation.33 | custom fusion | flops 393216 | bytes 1179648 | tf_op jit(solution)/shard_map/scatter-add | solution.py:79
  48.3 0.0 copy-done.1
  48.3 0.4 fusion.11
  48.7 1.3 collective-permute-start
  50.0 4.2 %collective-permute-start.1 = (bf16[1,2,768]{2,1,0:T(2,128)(2,1)S(1)}, bf16[1,2,768]{2,1,0:T(2,128)(2,1)S(1)}, u32[]{:S(2)}, u32[]{:S(2)}) collective-permute-start(bf16[1,2,768]{2,1,0:T(2,128)(2,1)S(1)} %get-tuple-element.2), channel_id=1, source_target_pairs={{0,1},{2,3},{4,5},{6,7},{8,9},{10,11},{12,13},{14,15},{16,17},{18,... | collective-permute-start | bytes 9224 | tf_op jit(solution)/shard_map/ppermute | solution.py:16
  54.1 127.4 %all-reduce.2.cloned.1.call-done = f32[768,768]{1,0:T(8,128)} async-done(((f32[768,768]{1,0:T(8,128)}), f32[768,768]{1,0:T(8,128)}) %all-reduce.2.cloned.1.call-update) | async-done | bytes 2359312 | tf_op jit(solution)/shard_map/psum | solution.py:91
  181.6 3.3 %broadcast_multiply_fusion = f32[768,768]{1,0:T(8,128)} fusion(f32[768,768]{1,0:T(8,128)} %all-reduce.2.cloned.1.call-done), kind=kLoop, calls=%fused_computation.23 | loop fusion | flops 589824 | bytes 4718592 | tf_op jit(solution)/shard_map/mul | solution.py:93
  184.8 0.0 collective-permute-done
  184.8 0.0 all-gather.2.cloned.1.call-done
  184.8 0.0 copy-start.2
  184.8 1.9 fusion.2
  186.8 1.9 convolution_add_fusion.3
  188.7 0.0 copy-done.2
  188.7 0.5 convolution_add_fusion.2
  189.2 0.0 collective-permute-done.1
  189.2 0.5 convolution_add_fusion.1
  189.8 1.3 fusion.1
  (5 shorter events, 0.1 us)
Async XLA Ops:
  8.0 23.8 %copy-start = (bf16[768,768]{1,0:T(8,128)(2,1)S(1)}, bf16[768,768]{1,0:T(8,128)(2,1)}, u32[]{:S(2)}) copy-start(bf16[768,768]{1,0:T(8,128)(2,1)} %param.11) | copy-start | bytes 3538948
  9.3 6.3 %copy-start.4 = (s32[1,1,2,128]{3,2,1,0:T(2,128)S(1)}, s32[1,1,2,128]{3,2,1,0:T(2,128)}, u32[]{:S(2)}) copy-start(s32[1,1,2,128]{3,2,1,0:T(2,128)} %param.13) | copy-start | bytes 3076
  11.9 4.9 %copy-start.5 = (s32[1,2,2]{2,1,0:T(2,128)S(1)}, s32[1,2,2]{2,1,0:T(2,128)}, u32[]{:S(2)}) copy-start(s32[1,2,2]{2,1,0:T(2,128)} %param.15) | copy-start | bytes 52
  11.9 5.1 %copy-start.6 = (f32[1,1,2,128]{3,2,1,0:T(2,128)S(1)}, f32[1,1,2,128]{3,2,1,0:T(2,128)}, u32[]{:S(2)}) copy-start(f32[1,1,2,128]{3,2,1,0:T(2,128)} %param.14) | copy-start | bytes 3076
  11.9 10.5 %all-to-all-start.1 = ((bf16[2,128,768]{2,1,0:T(8,128)(2,1)}), bf16[2,128,768]{2,1,0:T(8,128)(2,1)S(1)}, u32[]{:S(2)}, u32[]{:S(2)}) async-start(bf16[2,128,768]{2,1,0:T(8,128)(2,1)} %bitcast.9), calls=%async_computation.1 | async-start | bytes 786432 | tf_op jit(solution)/shard_map/all_to_all | solution.py:51
  15.5 166.0 %all-reduce.2.cloned.1.call-start = ((), (), s32[]{:S(2)}) async-start(), calls=%async_computation.4 | async-start | bytes 4718592 | tf_op jit(solution)/shard_map/psum | solution.py:91
  22.4 2.6 %copy-start.3 = (bf16[1,256,384]{2,1,0:T(8,128)(2,1)S(1)}, bf16[1,256,384]{2,1,0:T(8,128)(2,1)}, u32[]{:S(2)}) copy-start(bf16[1,256,384]{2,1,0:T(8,128)(2,1)} %param.9) | copy-start | bytes 589828
  24.4 160.4 %all-gather.2.cloned.1.call-start = ((), (), s32[]{:S(2)}) async-start(), calls=%async_computation.3 | async-start | bytes 6266880 | tf_op jit(solution)/shard_map/all_gather | solution.py:83
  28.4 7.4 %all-to-all-start = ((bf16[2,2,24576]{2,1,0:T(2,128)(2,1)}), bf16[2,2,24576]{2,1,0:T(2,128)(2,1)S(1)}, u32[]{:S(2)}, u32[]{:S(2)}) async-start(bf16[2,2,24576]{2,1,0:T(2,128)(2,1)} %reshape.152), calls=%async_computation | async-start | bytes 393216 | tf_op jit(solution)/shard_map/all_to_all | solution.py:47
  35.8 9.5 %all-to-all-start.2 = ((bf16[2,128,768]{2,1,0:T(8,128)(2,1)}), bf16[2,128,768]{2,1,0:T(8,128)(2,1)}, u32[]{:S(2)}, u32[]{:S(2)}) async-start(bf16[2,128,768]{2,1,0:T(8,128)(2,1)} %bitcast.13), calls=%async_computation.2 | async-start | bytes 786432 | tf_op jit(solution)/shard_map/all_to_all | solution.py:68
  41.9 6.4 %copy-start.1 = (bf16[1,256,768]{2,1,0:T(8,128)(2,1)S(1)}, bf16[1,256,768]{2,1,0:T(8,128)(2,1)}, u32[]{:S(2)}) copy-start(bf16[1,256,768]{2,1,0:T(8,128)(2,1)} %param.8) | copy-start | bytes 1179652
  48.7 136.2 %collective-permute-start = (bf16[1,2,768]{2,1,0:T(2,128)(2,1)S(1)}, bf16[1,2,768]{2,1,0:T(2,128)(2,1)S(1)}, u32[]{:S(2)}, u32[]{:S(2)}) collective-permute-start(bf16[1,2,768]{2,1,0:T(2,128)(2,1)S(1)} %get-tuple-element.3), channel_id=1, source_target_pairs={{1,0},{3,2},{5,4},{7,6},{9,8},{11,10},{13,12},{15,14},{17,16},{19,... | collective-permute-start | bytes 9224 | tf_op jit(solution)/shard_map/ppermute | solution.py:17
  50.0 139.3 %collective-permute-start.1 = (bf16[1,2,768]{2,1,0:T(2,128)(2,1)S(1)}, bf16[1,2,768]{2,1,0:T(2,128)(2,1)S(1)}, u32[]{:S(2)}, u32[]{:S(2)}) collective-permute-start(bf16[1,2,768]{2,1,0:T(2,128)(2,1)S(1)} %get-tuple-element.2), channel_id=1, source_target_pairs={{0,1},{2,3},{4,5},{6,7},{8,9},{10,11},{12,13},{14,15},{16,17},{18,... | collective-permute-start | bytes 9224 | tf_op jit(solution)/shard_map/ppermute | solution.py:16
  184.8 3.9 %copy-start.2 = (bf16[5,768,768]{2,1,0:T(8,128)(2,1)S(1)}, bf16[5,768,768]{2,1,0:T(8,128)(2,1)}, u32[]{:S(2)}) copy-start(bf16[5,768,768]{2,1,0:T(8,128)(2,1)} %all-gather.2.cloned.1.call-done) | copy-start | bytes 17694724
Sparse Core Ops, SparseCore 0:
  24.5 156.9 all-reduce.1
Sparse Core Ops, SparseCore 1:
  27.2 65.0 all-gather.1
where the time goes:
time: 200 us; the launch traced here: 198 us
  waiting for transfers between devices  137 us (68%)
  starting transfers between devices  16.7 us (8%)
  between operations  15.8 us (8%)
  other arithmetic  13.1 us (7%)
  matrix products  9.85 us (5%)
  local copies, waits for them, and re-layouts  6.27 us (3%)
    psum x1, waiting for transfers between devices, per_device(): pair_sum = lax.psum(pair_part, ('dp', 'seq'))  127 us
    dot_general x5, matrix products, per_device(): lax.dot_general(window, piece[tap], (((1,), (1,)), ((), ())), preferred_e...  6.12 us
    scatter-add x2, other arithmetic, per_device(): act_grad = pooled.at[accept_index].add(accept_term).at[send_index].add(re...  5.57 us
    all_to_all x1, waiting for transfers between devices, per_device(): lax.all_to_all(outgoing, 'seq', split_axis=0, concat_axis=0, tiled=True)  5.31 us
    all_to_all x1, starting transfers between devices, per_device(): lax.all_to_all(donor_term.reshape(seq_count, slot_count, channels), 'seq'...  4.17 us
    ppermute x1, starting transfers between devices, with_halo(): before = lax.ppermute(last, axis, up)  4.16 us
  transfers between devices with their start and end apart: 7, of which 4 were waited for; matrix products, arithmetic and copies ran while one was open for 11% of the time, Pallas kernels for 0%

commit v1 on v0

--- a/solution.py
+++ b/solution.py
@@ -3,6 +3,8 @@
 import jax
 import jax.numpy as jnp
 from jax import lax
+from jax.experimental import pallas as pl
+from jax.experimental.pallas import tpu as pltpu
 from jax.sharding import PartitionSpec as P
 
 
@@ -25,7 +27,7 @@
     return (values * normal_cdf, normal_cdf + values * density)
 
 
-def per_device(
+def per_device_general(
     pre_act,
     trunk_grad,
     conv_weight,
@@ -93,6 +95,298 @@
     return (input_grad[None], pair_sum * scale)
 
 
+MESH = pl.DeviceIdType.MESH
+NZ, NY, NC = 4, 2, 2
+ROWS_T = (((0,), (0,)), ((), ()))
+COLS_T = (((1,), (1,)), ((), ()))
+
+
+def dot(a, b):
+    return jnp.dot(a, b, preferred_element_type=jnp.float32)
+
+
+def kernel(
+    pre_ref, trunk_ref, w_ref, p_ref, ds_ref, as_ref, jg_ref, pc_ref,
+    out_ref, pair_ref,
+    act_s, slope_s, wbuf, trunk_in, dsend, drecv, tsend, trecv, drows, weighted_s, zbuf,
+    pad_s, halo_send, halo_recv, part_s, c_send, c_recv, x_send, x_recv, own_s, r_send, r_recv,
+    final,
+    wz_s, wz_r, wy_s, wy_r, wc_s, wc_r, loc_sem, xs_s, xs_r, ar_s, ar_r, rs_s, rs_r, ag_s, ag_r,
+):
+    dp = lax.axis_index("dp")
+    x = lax.axis_index("seq")
+    c = dp % 2
+    y = (dp // 2) % 2
+    z = dp // 4
+    me8 = dp // 2
+    ox = 1 - x
+    oc = 1 - c
+    chan = pre_ref.shape[2]
+    slots = ds_ref.shape[-1]
+    shard = w_ref.shape[1]
+    hc = chan // 2
+    slab = pre_ref.shape[1]
+    tok = slab // 2
+
+    def dev(zz, yy, cc):
+        return (zz * NY + yy) * NC + cc
+
+    def peer8(k):
+        return lax.rem(me8 + k, 8)
+
+    barrier = pltpu.get_barrier_semaphore()
+    for k in range(1, 8):
+        pl.semaphore_signal(barrier, inc=1, device_id=(peer8(k) * 2 + c, x), device_id_type=MESH)
+    pl.semaphore_signal(barrier, inc=1, device_id=(me8 * 2 + oc, x), device_id_type=MESH)
+    pl.semaphore_signal(barrier, inc=1, device_id=(dp, ox), device_id_type=MESH)
+    pl.semaphore_wait(barrier, 9)
+
+    def remote(src, dst, ss, rs, target):
+        return pltpu.make_async_remote_copy(
+            src_ref=src, dst_ref=dst, send_sem=ss, recv_sem=rs,
+            device_id=target, device_id_type=MESH,
+        )
+
+    def wblock(index):
+        return wbuf.at[:, pl.ds(pl.multiple_of(index * shard, 16), shard), :]
+
+    xdev = (dp, ox)
+    cdev = (me8 * 2 + oc, x)
+    ydev = (dev(z, 1 - y, c), x)
+
+    trunk_copy = remote(
+        trunk_ref.at[0, pl.ds(pl.multiple_of(ox * tok, 16), tok), :], trunk_in,
+        xs_s.at[0], xs_r.at[0], xdev)
+    trunk_copy.start()
+    wz = [None]
+    for k in range(1, NZ):
+        cp = remote(w_ref, wblock(dp), wz_s.at[k], wz_r.at[k],
+                    (dev(lax.rem(z + k, NZ), y, c), x))
+        cp.start()
+        wz.append(cp)
+    wy = [remote(w_ref, wblock(dp), wy_s.at[0], wy_r.at[0], ydev)]
+    wy[0].start()
+    wcore = {}
+    wcore[0, 0] = remote(w_ref, wblock(dp), wc_s.at[0], wc_r.at[0], cdev)
+    wcore[0, 0].start()
+    own_w = pltpu.make_async_copy(w_ref, wblock(dp), loc_sem)
+    own_w.start()
+
+    def pass_z(k):
+        wz[k].wait_recv()
+        block = wblock(dev(lax.rem(z + NZ - k, NZ), y, c))
+        cp = remote(block, block, wy_s.at[k], wy_r.at[k], ydev)
+        cp.start()
+        wy.append(cp)
+        cp = remote(block, block, wc_s.at[k], wc_r.at[k], cdev)
+        cp.start()
+        wcore[0, k] = cp
+
+    def pass_y(k):
+        wy[k].wait_recv()
+        block = wblock(dev(lax.rem(z + NZ - k, NZ), 1 - y, c))
+        cp = remote(block, block, wc_s.at[4 + k], wc_r.at[4 + k], cdev)
+        cp.start()
+        wcore[1, k] = cp
+
+    act_f, slope = gelu_parts(pre_ref[0].astype(jnp.float32))
+    act_s[...] = act_f.astype(jnp.bfloat16)
+    slope_s[...] = slope
+
+    first = x == 0
+
+    def loc_oth(rows):
+        a, b = rows[0:1], rows[1:2]
+        return jnp.where(first, a, b), jnp.where(first, b, a)
+
+    d_loc, d_oth = loc_oth(ds_ref[0, 0])
+    a_loc, a_oth = loc_oth(as_ref[0, 0])
+    counts = pc_ref[0]
+    cnt = jnp.where(first, counts[:, 0:1], counts[:, 1:2])
+    live = lax.broadcasted_iota(jnp.int32, (2, slots), 1) < cnt
+    w_loc, w_oth = loc_oth(jnp.where(live, jg_ref[0, 0], 0.0))
+
+    position = lax.broadcasted_iota(jnp.int32, (slab, slots), 0)
+
+    def onehot(row):
+        return jnp.where(position == row, 1.0, 0.0)
+
+    td_oth, td_loc, ta_oth, ta_loc = [onehot(r) for r in (d_oth, d_loc, a_oth, a_loc)]
+
+    def flip(m):
+        return jnp.transpose(m).astype(jnp.bfloat16)
+
+    def column(row):
+        return jnp.transpose(jnp.broadcast_to(row, (slots, slots)))[:, 0:1]
+
+    dsend[...] = dot(flip(td_oth), act_s[...]).astype(jnp.bfloat16)
+    d_copy = remote(dsend, drecv, xs_s.at[1], xs_r.at[1], xdev)
+    d_copy.start()
+
+    wc_oth, wc_loc = column(w_oth), column(w_loc)
+    rows = dot(flip(ta_oth), act_s[...])
+    weighted_s[0:slots, :] = (wc_oth * rows).astype(jnp.bfloat16)
+    tsend[...] = lax.dot_general(
+        weighted_s[0:slots, :], p_ref[...], COLS_T, preferred_element_type=jnp.float32
+    ).astype(jnp.bfloat16)
+    t_copy = remote(tsend, trecv, xs_s.at[2], xs_r.at[2], xdev)
+    t_copy.start()
+
+    rows = dot(flip(ta_loc), act_s[...])
+    weighted_s[slots:, :] = (wc_loc * rows).astype(jnp.bfloat16)
+    zbuf[3 * slots : 4 * slots, :] = lax.dot_general(
+        weighted_s[slots:, :], p_ref[...], COLS_T, preferred_element_type=jnp.float32
+    ).astype(jnp.bfloat16)
+    drows[slots:, :] = dot(flip(td_loc), act_s[...]).astype(jnp.bfloat16)
+    zbuf[slots : 2 * slots, :] = (
+        dot(drows[slots:, :], p_ref[...]) * wc_loc
+    ).astype(jnp.bfloat16)
+
+    d_copy.wait_recv()
+    drows[0:slots, :] = drecv[...]
+    part_s[...] = lax.dot_general(
+        drows[...], weighted_s[...], ROWS_T, preferred_element_type=jnp.float32)
+    c_send[...] = part_s[pl.ds(pl.multiple_of(oc * hc, 8), hc), :].astype(jnp.bfloat16)
+    c_copy = remote(c_send, c_recv, ar_s.at[0], ar_r.at[0], cdev)
+    c_copy.start()
+    zbuf[0:slots, :] = (dot(drows[0:slots, :], p_ref[...]) * wc_oth).astype(jnp.bfloat16)
+
+    trunk_copy.wait_recv()
+    mine = trunk_ref[0, pl.ds(pl.multiple_of(x * tok, 16), tok), :]
+    zbuf[4 * slots :, 0:hc] = jnp.where(first, mine, trunk_in[...])
+    zbuf[4 * slots :, hc:] = jnp.where(first, trunk_in[...], mine)
+    t_copy.wait_recv()
+    zbuf[2 * slots : 3 * slots, :] = trecv[...]
+    spread = jnp.where(
+        lax.broadcasted_iota(jnp.int32, (slab, tok), 0) // 2
+        == lax.broadcasted_iota(jnp.int32, (slab, tok), 1), 0.5, 0.0)
+    scatter = jnp.concatenate([ta_oth, ta_loc, td_oth, td_loc, spread], axis=1).astype(jnp.bfloat16)
+    grad = (dot(scatter, zbuf[...]) * slope_s[...]).astype(jnp.bfloat16).astype(jnp.float32)
+    pad_s[8 : 8 + slab, :] = grad
+    halo_send[0:8, :] = grad[0:8]
+    halo_send[8:16, :] = grad[slab - 8 : slab]
+    h_copy = remote(halo_send, halo_recv, xs_s.at[3], xs_r.at[3], xdev)
+    h_copy.start()
+
+    c_copy.wait_recv()
+    half = part_s[pl.ds(pl.multiple_of(c * hc, 8), hc), :] + c_recv[...].astype(jnp.float32)
+    left, right = half[:, 0:hc], half[:, hc:]
+    own_s[...] = jnp.where(first, left, right)
+    x_send[...] = jnp.where(first, right, left).astype(jnp.bfloat16)
+    x_copy = remote(x_send, x_recv, ar_s.at[1], ar_r.at[1], xdev)
+    x_copy.start()
+
+    pass_z(1)
+
+    h_copy.wait_recv()
+    nothing = jnp.zeros((8, chan), jnp.float32)
+    pad_s[0:8, :] = jnp.where(first, nothing, halo_recv[8:16, :])
+    pad_s[8 + slab :, :] = jnp.where(first, halo_recv[0:8, :], nothing)
+
+    x_copy.wait_recv()
+    own_s[...] = own_s[...] + x_recv[...].astype(jnp.float32)
+    r_send[...] = own_s[...].astype(jnp.bfloat16)
+    piece = hc // 8
+    rs = []
+    for k in range(1, 8):
+        to = peer8(k)
+        cp = remote(r_send.at[pl.ds(pl.multiple_of(to * piece, 16), piece), :], r_recv.at[k - 1],
+                    rs_s.at[k - 1], rs_r.at[k - 1], (to * 2 + c, x))
+        cp.start()
+        rs.append(cp)
+
+    pass_z(2)
+    pass_z(3)
+    for cp in rs:
+        cp.wait_recv()
+    total = own_s[pl.ds(pl.multiple_of(me8 * piece, 8), piece), :]
+    for k in range(7):
+        total = total + r_recv[k].astype(jnp.float32)
+
+    def fblock(cc, xx, start, size):
+        return final.at[pl.ds(pl.multiple_of(cc * hc + start, 16), size),
+                        pl.ds(pl.multiple_of(xx * hc, 128), hc)]
+
+    r_done = r_send
+    for cp in rs:
+        cp.wait_send()
+    r_done[0:piece, :] = total.astype(jnp.bfloat16)
+    mine_to = pltpu.make_async_copy(
+        r_done.at[0:piece, :], fblock(c, x, me8 * piece, piece), ar_s.at[5])
+    mine_to.start()
+    ag = []
+    for k in range(1, 8):
+        cp = remote(r_done.at[0:piece, :], fblock(c, x, me8 * piece, piece),
+                    ag_s.at[k - 1], ag_r.at[k - 1], (peer8(k) * 2 + c, x))
+        cp.start()
+        ag.append(cp)
+
+    pass_y(0)
+    pass_y(1)
+    mine_to.wait()
+    for cp in ag:
+        cp.wait_recv()
+    quarter = fblock(c, x, 0, hc)
+    xq = remote(quarter, quarter, ar_s.at[2], ar_r.at[2], xdev)
+    xq.start()
+    cq = remote(quarter, quarter, ar_s.at[3], ar_r.at[3], cdev)
+    cq.start()
+    pass_y(2)
+    pass_y(3)
+    xq.wait_recv()
+    other = fblock(c, ox, 0, hc)
+    cq2 = remote(other, other, ar_s.at[4], ar_r.at[4], cdev)
+    cq2.start()
+
+    own_w.wait()
+    for cp in wcore.values():
+        cp.wait_recv()
+    kernel_w = w_ref.shape[0]
+    shift = kernel_w // 2
+    acc = None
+    for tap in range(kernel_w):
+        window = pad_s[8 + shift - tap : 8 + shift - tap + slab, :].astype(jnp.bfloat16)
+        term = lax.dot_general(window, wbuf[tap], COLS_T, preferred_element_type=jnp.float32)
+        acc = term if acc is None else acc + term
+    out_ref[0] = acc.astype(jnp.bfloat16)
+
+    cq.wait_recv()
+    cq2.wait_recv()
+    scale = 1.0 / math.sqrt(NZ * NY * NC * 2 * 2 * slots)
+    pair_ref[...] = final[...].astype(jnp.float32) * scale
+    for cp in wz[1:] + wy + list(wcore.values()) + [trunk_copy, d_copy, t_copy, h_copy, c_copy, x_copy, xq, cq, cq2] + ag:
+        cp.wait_send()
+
+
+def per_device_kernel(pre_act, trunk_grad, conv_weight, pair_weight, donor_slots, accept_slots, junction_grad, pair_counts):
+    slab, chan = pre_act.shape[1:]
+    slots = donor_slots.shape[3]
+    hc = chan // 2
+    bf, f32 = jnp.bfloat16, jnp.float32
+    V = pltpu.VMEM
+    D = pltpu.SemaphoreType.DMA
+    scratch = [
+        V((slab, chan), bf), V((slab, chan), f32), V((conv_weight.shape[0], chan, chan), bf),
+        V((slab // 2, hc), bf), V((slots, chan), bf), V((slots, chan), bf),
+        V((slots, chan), bf), V((slots, chan), bf), V((2 * slots, chan), bf),
+        V((2 * slots, chan), bf), V((4 * slots + slab // 2, chan), bf),
+        V((slab + 16, chan), f32), V((16, chan), f32), V((16, chan), f32),
+        V((chan, chan), f32), V((hc, chan), bf), V((hc, chan), bf), V((hc, hc), bf), V((hc, hc), bf),
+        V((hc, hc), f32), V((hc, hc), bf), V((7, hc // 8, hc), bf), V((chan, chan), bf),
+        D((4,)), D((4,)), D((4,)), D((4,)), D((8,)), D((8,)), D, D((4,)), D((4,)),
+        D((6,)), D((6,)), D((7,)), D((7,)), D((7,)), D((7,)),
+    ]
+    return pl.pallas_call(
+        kernel,
+        out_shape=(jax.ShapeDtypeStruct(pre_act.shape, bf), jax.ShapeDtypeStruct((chan, chan), f32)),
+        in_specs=[pl.BlockSpec(memory_space=pltpu.VMEM)] * 8,
+        out_specs=[pl.BlockSpec(memory_space=pltpu.VMEM)] * 2,
+        scratch_shapes=scratch,
+        compiler_params=pltpu.CompilerParams(
+            collective_id=0, has_side_effects=True, vmem_limit_bytes=48 << 20),
+    )(pre_act, trunk_grad, conv_weight, pair_weight, donor_slots, accept_slots, junction_grad, pair_counts)
+
+
 def solution(mesh):
     in_specs = (
         P("dp", "seq", None),
@@ -105,6 +399,7 @@
         P("dp", None, None),
     )
     out_specs = (P("dp", "seq", None), P())
+    fits = mesh.shape["dp"] == NZ * NY * NC and mesh.shape["seq"] == 2
     return jax.shard_map(
-        per_device, mesh=mesh, in_specs=in_specs, out_specs=out_specs, check_vma=False
-    )
+        per_device_kernel if fits else per_device_general, mesh=mesh, in_specs=in_specs, out_specs=out_specs, check_vma=False
+    )

time: 200 us -> 79.1 us (0.40)
  the two profiles are of different devices: /device:TPU:1 before, /device:TPU:24 now
where the time goes in v1:
time: 79.1 us; the launch traced here: 78.8 us
  Pallas kernels  69.1 us (87%)
  local copies, waits for them, and re-layouts  9.04 us (11%)
    pallas_call x1, Pallas kernels, per_device_kernel(): pl.pallas_call(kernel, out_shape=(jax.ShapeDtypeStruct(pre_act.shape, bf)...  69.1 us
    unnamed x18, local copies, waits for them, and re-layouts  9.04 us

profile of v1, /device:TPU:24, one launch (start us, length us, event | category | flops | bytes accessed | tf_op | source)
XLA Modules:
  0.0 78.8 jit_solution(7399986551813156126)
XLA Ops:
  0.6 0.0 copy-start
  0.6 1.3 %copy-done = bf16[768,768]{1,0:T(8,128)(2,1)S(1)} copy-done((bf16[768,768]{1,0:T(8,128)(2,1)S(1)}, bf16[768,768]{1,0:T(8,128)(2,1)}, u32[]{:S(2)}) %copy-start) | copy-done | bytes 1179672
  1.9 0.0 copy-start.1
  1.9 1.0 %copy-done.1 = bf16[1,256,768]{2,1,0:T(8,128)(2,1)S(1)} copy-done((bf16[1,256,768]{2,1,0:T(8,128)(2,1)S(1)}, bf16[1,256,768]{2,1,0:T(8,128)(2,1)}, u32[]{:S(2)}) %copy-start.1) | copy-done | bytes 393240
  2.9 0.0 copy-start.2
  2.9 1.0 %copy-done.2 = bf16[5,48,768]{2,1,0:T(8,128)(2,1)S(1)} copy-done((bf16[5,48,768]{2,1,0:T(8,128)(2,1)S(1)}, bf16[5,48,768]{2,1,0:T(8,128)(2,1)}, u32[]{:S(2)}) %copy-start.2) | copy-done | bytes 368664
  3.9 0.0 copy-start.3
  3.9 0.9 %copy-done.3 = bf16[1,256,384]{2,1,0:T(8,128)(2,1)S(1)} copy-done((bf16[1,256,384]{2,1,0:T(8,128)(2,1)S(1)}, bf16[1,256,384]{2,1,0:T(8,128)(2,1)}, u32[]{:S(2)}) %copy-start.3) | copy-done | bytes 196632
  4.8 0.0 copy-start.4
  4.8 0.7 copy-done.4
  5.5 0.0 copy-start.5
  5.5 0.7 copy-done.5
  6.2 0.0 copy-start.6
  6.2 0.7 copy-done.6
  6.9 0.0 copy-start.7
  6.9 0.7 copy-done.7
  7.5 69.1 %shard_map.95 = (bf16[1,256,768]{2,1,0:T(8,128)(2,1)S(1)}, f32[768,768]{1,0:T(8,128)S(1)}) custom-call(bf16[1,256,768]{2,1,0:T(8,128)(2,1)S(1)} %copy-done.1, bf16[1,256,384]{2,1,0:T(8,128)(2,1)S(1)} %copy-done.3, bf16[5,48,768]{2,1,0:T(8,128)(2,1)S(1)} %copy-done.2, bf16[768,768]{1,0:T(8,128)(2,1)S(1)} %copy-done, s32[1,1,2,128]{3,2,1,0:T(2,128)S(1)} %copy-done.4, ...), custom_call_target="tpu_custom_call" | custom-call | tf_op jit(solution)/shard_map/pallas_call | solution.py:379
  76.7 0.7 copy.12
  77.4 1.4 %copy.13 = f32[768,768]{1,0:T(8,128)} copy(f32[768,768]{1,0:T(8,128)S(1)} %get-tuple-element.5) | data formatting | bytes 4718592
Async XLA Ops:
  0.6 1.3 %copy-start = (bf16[768,768]{1,0:T(8,128)(2,1)S(1)}, bf16[768,768]{1,0:T(8,128)(2,1)}, u32[]{:S(2)}) copy-start(bf16[768,768]{1,0:T(8,128)(2,1)} %p_ref.1) | copy-start | bytes 3538948
  1.9 1.0 %copy-start.1 = (bf16[1,256,768]{2,1,0:T(8,128)(2,1)S(1)}, bf16[1,256,768]{2,1,0:T(8,128)(2,1)}, u32[]{:S(2)}) copy-start(bf16[1,256,768]{2,1,0:T(8,128)(2,1)} %pre_ref.1) | copy-start | bytes 1179652
  2.9 1.0 %copy-start.2 = (bf16[5,48,768]{2,1,0:T(8,128)(2,1)S(1)}, bf16[5,48,768]{2,1,0:T(8,128)(2,1)}, u32[]{:S(2)}) copy-start(bf16[5,48,768]{2,1,0:T(8,128)(2,1)} %w_ref.1) | copy-start | bytes 1105924
  3.9 0.9 %copy-start.3 = (bf16[1,256,384]{2,1,0:T(8,128)(2,1)S(1)}, bf16[1,256,384]{2,1,0:T(8,128)(2,1)}, u32[]{:S(2)}) copy-start(bf16[1,256,384]{2,1,0:T(8,128)(2,1)} %trunk_ref.1) | copy-start | bytes 589828
  4.8 0.7 copy-start.4
  5.5 0.7 copy-start.5
  6.2 0.7 copy-start.6
  6.9 0.7 copy-start.7

commit v2 on v1

--- a/solution.py
+++ b/solution.py
@@ -97,6 +97,7 @@
 
 MESH = pl.DeviceIdType.MESH
 NZ, NY, NC = 4, 2, 2
+Y_TAPS = 4
 ROWS_T = (((0,), (0,)), ((), ()))
 COLS_T = (((1,), (1,)), ((), ()))
 
@@ -106,12 +107,13 @@
 
 
 def kernel(
-    pre_ref, trunk_ref, w_ref, p_ref, ds_ref, as_ref, jg_ref, pc_ref,
+    pre_hbm, trunk_ref, w_ref, p_hbm, ds_hbm, as_hbm, jg_hbm, pc_hbm,
     out_ref, pair_ref,
+    pre_ref, p_ref, ds_ref, as_ref, jg_ref, pc_ref, trunk_mine, in_sem,
     act_s, slope_s, wbuf, trunk_in, dsend, drecv, tsend, trecv, drows, weighted_s, zbuf,
     pad_s, halo_send, halo_recv, part_s, c_send, c_recv, x_send, x_recv, own_s, r_send, r_recv,
     final,
-    wz_s, wz_r, wy_s, wy_r, wc_s, wc_r, loc_sem, xs_s, xs_r, ar_s, ar_r, rs_s, rs_r, ag_s, ag_r,
+    wz_s, wz_r, wy_s, wy_r, wx_s, wx_r, wc_s, wc_r, xs_s, xs_r, ar_s, ar_r, rs_s, rs_r, ag_s, ag_r,
 ):
     dp = lax.axis_index("dp")
     x = lax.axis_index("seq")
@@ -131,6 +133,16 @@
     def dev(zz, yy, cc):
         return (zz * NY + yy) * NC + cc
 
+    loads = [
+        pltpu.make_async_copy(src, dst, in_sem.at[i])
+        for i, (src, dst) in enumerate([
+            (pre_hbm, pre_ref), (ds_hbm, ds_ref), (as_hbm, as_ref), (jg_hbm, jg_ref),
+            (pc_hbm, pc_ref), (p_hbm, p_ref),
+            (trunk_ref.at[0, pl.ds(pl.multiple_of(x * tok, 16), tok), :], trunk_mine)])
+    ]
+    for cp in loads:
+        cp.start()
+
     def peer8(k):
         return lax.rem(me8 + k, 8)
 
@@ -147,48 +159,107 @@
             device_id=target, device_id_type=MESH,
         )
 
-    def wblock(index):
-        return wbuf.at[:, pl.ds(pl.multiple_of(index * shard, 16), shard), :]
+    def wpart(ref, index, first_tap, taps):
+        return ref.at[pl.ds(first_tap, taps), pl.ds(pl.multiple_of(index * shard, 16), shard), :]
 
     xdev = (dp, ox)
     cdev = (me8 * 2 + oc, x)
     ydev = (dev(z, 1 - y, c), x)
+    taps = w_ref.shape[0]
+    x_taps = taps - Y_TAPS
 
     trunk_copy = remote(
         trunk_ref.at[0, pl.ds(pl.multiple_of(ox * tok, 16), tok), :], trunk_in,
         xs_s.at[0], xs_r.at[0], xdev)
     trunk_copy.start()
-    wz = [None]
-    for k in range(1, NZ):
-        cp = remote(w_ref, wblock(dp), wz_s.at[k], wz_r.at[k],
-                    (dev(lax.rem(z + k, NZ), y, c), x))
-        cp.start()
-        wz.append(cp)
-    wy = [remote(w_ref, wblock(dp), wy_s.at[0], wy_r.at[0], ydev)]
-    wy[0].start()
-    wcore = {}
-    wcore[0, 0] = remote(w_ref, wblock(dp), wc_s.at[0], wc_r.at[0], cdev)
-    wcore[0, 0].start()
-    own_w = pltpu.make_async_copy(w_ref, wblock(dp), loc_sem)
+
+    hops = [(d, s) for s in range(NZ - 1) for d in range(2)]
+
+    def entry(hop):
+        return 0 if hop is None else 1 + hop[0] * 3 + hop[1]
+
+    def source_z(hop):
+        if hop is None:
+            return z
+        return z - 1 - hop[1] if hop[0] == 0 else z + 1 + hop[1]
+
+    def present(hop):
+        return source_z(hop) >= 0 if hop[0] == 0 else source_z(hop) < NZ
+
+    def when(hop, body):
+        if hop is None:
+            body()
+        else:
+            pl.when(present(hop))(body)
+
+    def z_copy(d, s):
+        block = wpart(wbuf, dev(z - s if d == 0 else z + s, y, c), 0, taps)
+        return remote(w_ref if s == 0 else block, block, wz_s.at[d * 3 + s], wz_r.at[d * 3 + s],
+                      (dev(z + 1 if d == 0 else z - 1, y, c), x))
+
+    def z_arrival(d, s):
+        block = wpart(wbuf, dev(source_z((d, s)), y, c), 0, taps)
+        return remote(block, block, wz_s.at[d * 3 + s], wz_r.at[d * 3 + s], ydev)
+
+    def has_next(d):
+        return z < NZ - 1 if d == 0 else z > 0
+
+    def y_copy(hop, arriving=False):
+        index = dev(source_z(hop), 1 - y if arriving else y, c)
+        block = wpart(wbuf, index, x * x_taps, Y_TAPS)
+        src = w_ref.at[pl.ds(x * x_taps, Y_TAPS)] if hop is None and not arriving else block
+        return remote(src, block, wy_s.at[entry(hop)], wy_r.at[entry(hop)], ydev)
+
+    def x_copy_w(hop, arriving=False):
+        start = (ox if arriving else x) * Y_TAPS
+        block = wpart(wbuf, dev(source_z(hop), 1 - y, c), start, x_taps)
+        return remote(block, block, wx_s.at[entry(hop)], wx_r.at[entry(hop)], xdev)
+
+    def core_copy(kind, hop, arriving=False):
+        yy, first_tap, count = [
+            (y, 0, taps), (1 - y, x * x_taps, Y_TAPS), (1 - y, ox * Y_TAPS, x_taps)][kind]
+        block = wpart(wbuf, dev(source_z(hop), yy, oc if arriving else c), first_tap, count)
+        src = w_ref if kind == 0 and hop is None and not arriving else block
+        sem = kind * 7 + entry(hop)
+        return remote(src, block, wc_s.at[sem], wc_r.at[sem], cdev)
+
+    for d in range(2):
+        @pl.when(has_next(d))
+        def _():
+            z_copy(d, 0).start()
+    y_copy(None).start()
+    core_copy(0, None).start()
+    own_w = pltpu.make_async_copy(w_ref, wpart(wbuf, dp, 0, taps), in_sem.at[7])
     own_w.start()
 
-    def pass_z(k):
-        wz[k].wait_recv()
-        block = wblock(dev(lax.rem(z + NZ - k, NZ), y, c))
-        cp = remote(block, block, wy_s.at[k], wy_r.at[k], ydev)
-        cp.start()
-        wy.append(cp)
-        cp = remote(block, block, wc_s.at[k], wc_r.at[k], cdev)
-        cp.start()
-        wcore[0, k] = cp
-
-    def pass_y(k):
-        wy[k].wait_recv()
-        block = wblock(dev(lax.rem(z + NZ - k, NZ), 1 - y, c))
-        cp = remote(block, block, wc_s.at[4 + k], wc_r.at[4 + k], cdev)
-        cp.start()
-        wcore[1, k] = cp
-
+    def pass_z(s):
+        for d in range(2):
+            def body(d=d):
+                z_arrival(d, s).wait_recv()
+                if s < NZ - 2:
+                    @pl.when(has_next(d))
+                    def _():
+                        z_copy(d, s + 1).start()
+                y_copy((d, s)).start()
+                core_copy(0, (d, s)).start()
+            when((d, s), body)
+
+    def pass_y(step):
+        for hop in [None] if step == 0 else [(0, step - 1), (1, step - 1)]:
+            def body(hop=hop):
+                y_copy(hop, True).wait_recv()
+                x_copy_w(hop).start()
+                core_copy(1, hop).start()
+            when(hop, body)
+
+    def pass_x(step):
+        for hop in [None] if step == 0 else [(0, step - 1), (1, step - 1)]:
+            def body(hop=hop):
+                x_copy_w(hop, True).wait_recv()
+                core_copy(2, hop).start()
+            when(hop, body)
+
+    loads[0].wait()
     act_f, slope = gelu_parts(pre_ref[0].astype(jnp.float32))
     act_s[...] = act_f.astype(jnp.bfloat16)
     slope_s[...] = slope
@@ -199,6 +270,8 @@
         a, b = rows[0:1], rows[1:2]
         return jnp.where(first, a, b), jnp.where(first, b, a)
 
+    for cp in loads[1:5]:
+        cp.wait()
     d_loc, d_oth = loc_oth(ds_ref[0, 0])
     a_loc, a_oth = loc_oth(as_ref[0, 0])
     counts = pc_ref[0]
@@ -226,12 +299,14 @@
     wc_oth, wc_loc = column(w_oth), column(w_loc)
     rows = dot(flip(ta_oth), act_s[...])
     weighted_s[0:slots, :] = (wc_oth * rows).astype(jnp.bfloat16)
+    loads[5].wait()
     tsend[...] = lax.dot_general(
         weighted_s[0:slots, :], p_ref[...], COLS_T, preferred_element_type=jnp.float32
     ).astype(jnp.bfloat16)
     t_copy = remote(tsend, trecv, xs_s.at[2], xs_r.at[2], xdev)
     t_copy.start()
 
+    pass_z(0)
     rows = dot(flip(ta_loc), act_s[...])
     weighted_s[slots:, :] = (wc_loc * rows).astype(jnp.bfloat16)
     zbuf[3 * slots : 4 * slots, :] = lax.dot_general(
@@ -249,10 +324,12 @@
     c_send[...] = part_s[pl.ds(pl.multiple_of(oc * hc, 8), hc), :].astype(jnp.bfloat16)
     c_copy = remote(c_send, c_recv, ar_s.at[0], ar_r.at[0], cdev)
     c_copy.start()
+    pass_y(0)
     zbuf[0:slots, :] = (dot(drows[0:slots, :], p_ref[...]) * wc_oth).astype(jnp.bfloat16)
 
     trunk_copy.wait_recv()
-    mine = trunk_ref[0, pl.ds(pl.multiple_of(x * tok, 16), tok), :]
+    loads[6].wait()
+    mine = trunk_mine[...]
     zbuf[4 * slots :, 0:hc] = jnp.where(first, mine, trunk_in[...])
     zbuf[4 * slots :, hc:] = jnp.where(first, trunk_in[...], mine)
     t_copy.wait_recv()
@@ -268,6 +345,8 @@
     h_copy = remote(halo_send, halo_recv, xs_s.at[3], xs_r.at[3], xdev)
     h_copy.start()
 
+    pass_z(1)
+    pass_x(0)
     c_copy.wait_recv()
     half = part_s[pl.ds(pl.multiple_of(c * hc, 8), hc), :] + c_recv[...].astype(jnp.float32)
     left, right = half[:, 0:hc], half[:, hc:]
@@ -276,7 +355,7 @@
     x_copy = remote(x_send, x_recv, ar_s.at[1], ar_r.at[1], xdev)
     x_copy.start()
 
-    pass_z(1)
+    pass_y(1)
 
     h_copy.wait_recv()
     nothing = jnp.zeros((8, chan), jnp.float32)
@@ -296,7 +375,8 @@
         rs.append(cp)
 
     pass_z(2)
-    pass_z(3)
+    pass_x(1)
+    pass_y(2)
     for cp in rs:
         cp.wait_recv()
     total = own_s[pl.ds(pl.multiple_of(me8 * piece, 8), piece), :]
@@ -321,8 +401,6 @@
         cp.start()
         ag.append(cp)
 
-    pass_y(0)
-    pass_y(1)
     mine_to.wait()
     for cp in ag:
         cp.wait_recv()
@@ -331,16 +409,20 @@
     xq.start()
     cq = remote(quarter, quarter, ar_s.at[3], ar_r.at[3], cdev)
     cq.start()
-    pass_y(2)
+    pass_x(2)
     pass_y(3)
+    pass_x(3)
     xq.wait_recv()
     other = fblock(c, ox, 0, hc)
     cq2 = remote(other, other, ar_s.at[4], ar_r.at[4], cdev)
     cq2.start()
 
     own_w.wait()
-    for cp in wcore.values():
-        cp.wait_recv()
+    for hop in [None] + hops:
+        def arrived(hop=hop):
+            for kind in range(3):
+                core_copy(kind, hop, True).wait_recv()
+        when(hop, arrived)
     kernel_w = w_ref.shape[0]
     shift = kernel_w // 2
     acc = None
@@ -354,7 +436,20 @@
     cq2.wait_recv()
     scale = 1.0 / math.sqrt(NZ * NY * NC * 2 * 2 * slots)
     pair_ref[...] = final[...].astype(jnp.float32) * scale
-    for cp in wz[1:] + wy + list(wcore.values()) + [trunk_copy, d_copy, t_copy, h_copy, c_copy, x_copy, xq, cq, cq2] + ag:
+    for hop in [None] + hops:
+        def sent(hop=hop):
+            y_copy(hop).wait_send()
+            x_copy_w(hop).wait_send()
+            for kind in range(3):
+                core_copy(kind, hop).wait_send()
+        when(hop, sent)
+    for d in range(2):
+        for s in range(NZ - 1):
+            leaves = (z < NZ - 1) & (z >= s) if d == 0 else (z > 0) & (z + s < NZ)
+            @pl.when(leaves)
+            def _(d=d, s=s):
+                z_copy(d, s).wait_send()
+    for cp in [trunk_copy, d_copy, t_copy, h_copy, c_copy, x_copy, xq, cq, cq2] + ag:
         cp.wait_send()
 
 
@@ -366,6 +461,9 @@
     V = pltpu.VMEM
     D = pltpu.SemaphoreType.DMA
     scratch = [
+        V(pre_act.shape, bf), V(pair_weight.shape, bf), V(donor_slots.shape, jnp.int32),
+        V(accept_slots.shape, jnp.int32), V(junction_grad.shape, f32), V(pair_counts.shape, jnp.int32),
+        V((slab // 2, hc), bf), D((8,)),
         V((slab, chan), bf), V((slab, chan), f32), V((conv_weight.shape[0], chan, chan), bf),
         V((slab // 2, hc), bf), V((slots, chan), bf), V((slots, chan), bf),
         V((slots, chan), bf), V((slots, chan), bf), V((2 * slots, chan), bf),
@@ -373,17 +471,17 @@
         V((slab + 16, chan), f32), V((16, chan), f32), V((16, chan), f32),
         V((chan, chan), f32), V((hc, chan), bf), V((hc, chan), bf), V((hc, hc), bf), V((hc, hc), bf),
         V((hc, hc), f32), V((hc, hc), bf), V((7, hc // 8, hc), bf), V((chan, chan), bf),
-        D((4,)), D((4,)), D((4,)), D((4,)), D((8,)), D((8,)), D, D((4,)), D((4,)),
+        D((6,)), D((6,)), D((7,)), D((7,)), D((7,)), D((7,)), D((21,)), D((21,)), D((4,)), D((4,)),
         D((6,)), D((6,)), D((7,)), D((7,)), D((7,)), D((7,)),
     ]
     return pl.pallas_call(
         kernel,
         out_shape=(jax.ShapeDtypeStruct(pre_act.shape, bf), jax.ShapeDtypeStruct((chan, chan), f32)),
-        in_specs=[pl.BlockSpec(memory_space=pltpu.VMEM)] * 8,
+        in_specs=[pl.BlockSpec(memory_space=pltpu.HBM)] * 8,
         out_specs=[pl.BlockSpec(memory_space=pltpu.VMEM)] * 2,
         scratch_shapes=scratch,
         compiler_params=pltpu.CompilerParams(
-            collective_id=0, has_side_effects=True, vmem_limit_bytes=48 << 20),
+            collective_id=0, has_side_effects=True, vmem_limit_bytes=60 << 20),
     )(pre_act, trunk_grad, conv_weight, pair_weight, donor_slots, accept_slots, junction_grad, pair_counts)
 
 

time: 79.1 us -> 63.7 us (0.81)
  the two profiles are of different devices: /device:TPU:24 before, /device:TPU:1 now
where the time goes in v2:
time: 63.7 us; the launch traced here: 63.5 us
  Pallas kernels  57.8 us (91%)
  local copies, waits for them, and re-layouts  4.99 us (8%)
  between operations  0.64 us (1%)
    pallas_call x1, Pallas kernels, per_device_kernel(): pl.pallas_call(kernel, out_shape=(jax.ShapeDtypeStruct(pre_act.shape, bf)...  57.8 us
    unnamed x2, local copies, waits for them, and re-layouts  4.99 us

profile of v2, /device:TPU:1, one launch (start us, length us, event | category | flops | bytes accessed | tf_op | source)
XLA Modules:
  0.0 63.5 jit_solution(3036351789070213029)
XLA Ops:
  0.6 57.8 %shard_map.95 = (bf16[1,256,768]{2,1,0:T(8,128)(2,1)}, f32[768,768]{1,0:T(8,128)}) custom-call(bf16[1,256,768]{2,1,0:T(8,128)(2,1)} %pre_hbm.1, bf16[1,256,384]{2,1,0:T(8,128)(2,1)} %trunk_ref.1, bf16[5,48,768]{2,1,0:T(8,128)(2,1)} %w_ref.1, bf16[768,768]{1,0:T(8,128)(2,1)} %p_hbm.1, s32[1,1,2,128]{3,2,1,0:T(2,128)} %ds_hbm.1, s32[1,1,2,128]{3,2,1,0:T(2,128)} %as_hbm.1, ...), custom_call_target="tpu_custom_call" | custom-call | tf_op jit(solution)/shard_map/pallas_call | solution.py:477
  58.5 1.8 %copy.12 = bf16[1,256,768]{2,1,0:T(8,128)(2,1)} copy(bf16[1,256,768]{2,1,0:T(8,128)(2,1)} %get-tuple-element.4) | data formatting | bytes 786432
  60.2 3.2 %copy.13 = f32[768,768]{1,0:T(8,128)} copy(f32[768,768]{1,0:T(8,128)} %get-tuple-element.5) | data formatting | bytes 4718592

commit v3 on v2

--- a/solution.py
+++ b/solution.py
@@ -260,9 +260,10 @@
             when(hop, body)
 
     loads[0].wait()
-    act_f, slope = gelu_parts(pre_ref[0].astype(jnp.float32))
-    act_s[...] = act_f.astype(jnp.bfloat16)
-    slope_s[...] = slope
+    values = pre_ref[0].astype(jnp.float32)
+    normal_cdf = 0.5 * (1.0 + lax.erf(values / math.sqrt(2.0)))
+    act_s[...] = (values * normal_cdf).astype(jnp.bfloat16)
+    slope_s[...] = normal_cdf
 
     first = x == 0
 
@@ -299,34 +300,46 @@
     wc_oth, wc_loc = column(w_oth), column(w_loc)
     rows = dot(flip(ta_oth), act_s[...])
     weighted_s[0:slots, :] = (wc_oth * rows).astype(jnp.bfloat16)
+    rows = dot(flip(ta_loc), act_s[...])
+    weighted_s[slots:, :] = (wc_loc * rows).astype(jnp.bfloat16)
+    drows[slots:, :] = dot(flip(td_loc), act_s[...]).astype(jnp.bfloat16)
+    part_s[...] = lax.dot_general(
+        drows[slots:, :], weighted_s[slots:, :], ROWS_T, preferred_element_type=jnp.float32)
     loads[5].wait()
     tsend[...] = lax.dot_general(
         weighted_s[0:slots, :], p_ref[...], COLS_T, preferred_element_type=jnp.float32
     ).astype(jnp.bfloat16)
+
+    d_copy.wait_recv()
     t_copy = remote(tsend, trecv, xs_s.at[2], xs_r.at[2], xdev)
     t_copy.start()
-
+    drows[0:slots, :] = drecv[...]
+    part_s[...] += lax.dot_general(
+        drows[0:slots, :], weighted_s[0:slots, :], ROWS_T, preferred_element_type=jnp.float32)
+    c_send[...] = part_s[pl.ds(pl.multiple_of(oc * hc, 8), hc), :].astype(jnp.bfloat16)
+    c_copy = remote(c_send, c_recv, ar_s.at[0], ar_r.at[0], cdev)
+    c_copy.start()
     pass_z(0)
-    rows = dot(flip(ta_loc), act_s[...])
-    weighted_s[slots:, :] = (wc_loc * rows).astype(jnp.bfloat16)
     zbuf[3 * slots : 4 * slots, :] = lax.dot_general(
         weighted_s[slots:, :], p_ref[...], COLS_T, preferred_element_type=jnp.float32
     ).astype(jnp.bfloat16)
-    drows[slots:, :] = dot(flip(td_loc), act_s[...]).astype(jnp.bfloat16)
+    zbuf[0:slots, :] = (dot(drows[0:slots, :], p_ref[...]) * wc_oth).astype(jnp.bfloat16)
     zbuf[slots : 2 * slots, :] = (
         dot(drows[slots:, :], p_ref[...]) * wc_loc
     ).astype(jnp.bfloat16)
-
-    d_copy.wait_recv()
-    drows[0:slots, :] = drecv[...]
-    part_s[...] = lax.dot_general(
-        drows[...], weighted_s[...], ROWS_T, preferred_element_type=jnp.float32)
-    c_send[...] = part_s[pl.ds(pl.multiple_of(oc * hc, 8), hc), :].astype(jnp.bfloat16)
-    c_copy = remote(c_send, c_recv, ar_s.at[0], ar_r.at[0], cdev)
-    c_copy.start()
     pass_y(0)
-    zbuf[0:slots, :] = (dot(drows[0:slots, :], p_ref[...]) * wc_oth).astype(jnp.bfloat16)
-
+
+    c_copy.wait_recv()
+    half = part_s[pl.ds(pl.multiple_of(c * hc, 8), hc), :] + c_recv[...].astype(jnp.float32)
+    left, right = half[:, 0:hc], half[:, hc:]
+    x_send[...] = jnp.where(first, right, left).astype(jnp.bfloat16)
+    x_copy = remote(x_send, x_recv, ar_s.at[1], ar_r.at[1], xdev)
+    x_copy.start()
+    own_s[...] = jnp.where(first, left, right)
+
+    values = pre_ref[0].astype(jnp.float32)
+    density = jnp.exp(-0.5 * values * values) / math.sqrt(2.0 * math.pi)
+    slope_s[...] += values * density
     trunk_copy.wait_recv()
     loads[6].wait()
     mine = trunk_mine[...]
@@ -340,28 +353,12 @@
     scatter = jnp.concatenate([ta_oth, ta_loc, td_oth, td_loc, spread], axis=1).astype(jnp.bfloat16)
     grad = (dot(scatter, zbuf[...]) * slope_s[...]).astype(jnp.bfloat16).astype(jnp.float32)
     pad_s[8 : 8 + slab, :] = grad
-    halo_send[0:8, :] = grad[0:8]
-    halo_send[8:16, :] = grad[slab - 8 : slab]
+    halo_send[...] = jnp.where(first, grad[slab - 8 : slab], grad[0:8])
     h_copy = remote(halo_send, halo_recv, xs_s.at[3], xs_r.at[3], xdev)
     h_copy.start()
 
     pass_z(1)
     pass_x(0)
-    c_copy.wait_recv()
-    half = part_s[pl.ds(pl.multiple_of(c * hc, 8), hc), :] + c_recv[...].astype(jnp.float32)
-    left, right = half[:, 0:hc], half[:, hc:]
-    own_s[...] = jnp.where(first, left, right)
-    x_send[...] = jnp.where(first, right, left).astype(jnp.bfloat16)
-    x_copy = remote(x_send, x_recv, ar_s.at[1], ar_r.at[1], xdev)
-    x_copy.start()
-
-    pass_y(1)
-
-    h_copy.wait_recv()
-    nothing = jnp.zeros((8, chan), jnp.float32)
-    pad_s[0:8, :] = jnp.where(first, nothing, halo_recv[8:16, :])
-    pad_s[8 + slab :, :] = jnp.where(first, halo_recv[0:8, :], nothing)
-
     x_copy.wait_recv()
     own_s[...] = own_s[...] + x_recv[...].astype(jnp.float32)
     r_send[...] = own_s[...].astype(jnp.bfloat16)
@@ -374,9 +371,13 @@
         cp.start()
         rs.append(cp)
 
+    pass_y(1)
+    h_copy.wait_recv()
+    nothing = jnp.zeros((8, chan), jnp.float32)
+    pad_s[0:8, :] = jnp.where(first, nothing, halo_recv[...])
+    pad_s[8 + slab :, :] = jnp.where(first, halo_recv[...], nothing)
+
     pass_z(2)
-    pass_x(1)
-    pass_y(2)
     for cp in rs:
         cp.wait_recv()
     total = own_s[pl.ds(pl.multiple_of(me8 * piece, 8), piece), :]
@@ -401,6 +402,8 @@
         cp.start()
         ag.append(cp)
 
+    pass_x(1)
+    pass_y(2)
     mine_to.wait()
     for cp in ag:
         cp.wait_recv()
@@ -468,7 +471,7 @@
         V((slab // 2, hc), bf), V((slots, chan), bf), V((slots, chan), bf),
         V((slots, chan), bf), V((slots, chan), bf), V((2 * slots, chan), bf),
         V((2 * slots, chan), bf), V((4 * slots + slab // 2, chan), bf),
-        V((slab + 16, chan), f32), V((16, chan), f32), V((16, chan), f32),
+        V((slab + 16, chan), f32), V((8, chan), f32), V((8, chan), f32),
         V((chan, chan), f32), V((hc, chan), bf), V((hc, chan), bf), V((hc, hc), bf), V((hc, hc), bf),
         V((hc, hc), f32), V((hc, hc), bf), V((7, hc // 8, hc), bf), V((chan, chan), bf),
         D((6,)), D((6,)), D((7,)), D((7,)), D((7,)), D((7,)), D((21,)), D((21,)), D((4,)), D((4,)),
@@ -481,8 +484,12 @@
         out_specs=[pl.BlockSpec(memory_space=pltpu.VMEM)] * 2,
         scratch_shapes=scratch,
         compiler_params=pltpu.CompilerParams(
-            collective_id=0, has_side_effects=True, vmem_limit_bytes=60 << 20),
-    )(pre_act, trunk_grad, conv_weight, pair_weight, donor_slots, accept_slots, junction_grad, pair_counts)
+            collective_id=0, has_side_effects=True, vmem_limit_bytes=40 << 20),
+    )(*[
+        pltpu.with_memory_space_constraint(a, pltpu.HBM)
+        for a in (pre_act, trunk_grad, conv_weight, pair_weight, donor_slots, accept_slots,
+                  junction_grad, pair_counts)
+    ])
 
 
 def solution(mesh):

time: 63.7 us -> 59 us (0.926)
  local copies, waits for them, and re-layouts: 4.99 us -> 2.15 us
  Pallas kernels: 57.8 us -> 56.1 us
    unnamed x2, local copies, waits for them, and re-layouts: 4.99 us -> 2.15 us
    pallas_call x1, Pallas kernels: 57.8 us -> 56.1 us  [per_device_kernel(): pl.pallas_call(kernel, out_shape=(jax.ShapeDtypeStruct(pre_act.shape, bf)...]
where the time goes in v3:
time: 59 us; the launch traced here: 58.9 us
  Pallas kernels  56.1 us (95%)
  local copies, waits for them, and re-layouts  2.15 us (4%)
  between operations  0.64 us (1%)
    pallas_call x1, Pallas kernels, per_device_kernel(): pl.pallas_call(kernel, out_shape=(jax.ShapeDtypeStruct(pre_act.shape, bf)...  56.1 us
    unnamed x2, local copies, waits for them, and re-layouts  2.15 us

profile of v3, /device:TPU:1, one launch (start us, length us, event | category | flops | bytes accessed | tf_op | source)
XLA Modules:
  0.0 58.9 jit_solution(10735507107681602322)
XLA Ops:
  0.6 56.1 %shard_map.95 = (bf16[1,256,768]{2,1,0:T(8,128)(2,1)S(1)}, f32[768,768]{1,0:T(8,128)S(1)}) custom-call(bf16[1,256,768]{2,1,0:T(8,128)(2,1)} %pre_hbm.1, bf16[1,256,384]{2,1,0:T(8,128)(2,1)} %trunk_ref.1, bf16[5,48,768]{2,1,0:T(8,128)(2,1)} %w_ref.1, bf16[768,768]{1,0:T(8,128)(2,1)} %p_hbm.1, s32[1,1,2,128]{3,2,1,0:T(2,128)} %ds_hbm.1, ...), custom_call_target="tpu_custom_call" | custom-call | tf_op jit(solution)/shard_map/pallas_call | solution.py:480
  56.7 0.7 %copy.12 = bf16[1,256,768]{2,1,0:T(8,128)(2,1)} copy(bf16[1,256,768]{2,1,0:T(8,128)(2,1)S(1)} %get-tuple-element.4) | data formatting | bytes 786432
  57.5 1.4 %copy.13 = f32[768,768]{1,0:T(8,128)} copy(f32[768,768]{1,0:T(8,128)S(1)} %get-tuple-element.5) | data formatting | bytes 4718592

commit v4 on v3

--- a/solution.py
+++ b/solution.py
@@ -113,7 +113,7 @@
     act_s, slope_s, wbuf, trunk_in, dsend, drecv, tsend, trecv, drows, weighted_s, zbuf,
     pad_s, halo_send, halo_recv, part_s, c_send, c_recv, x_send, x_recv, own_s, r_send, r_recv,
     final,
-    wz_s, wz_r, wy_s, wy_r, wx_s, wx_r, wc_s, wc_r, xs_s, xs_r, ar_s, ar_r, rs_s, rs_r, ag_s, ag_r,
+    wz_s, wz_r, wy_s, wy_r, wx_s, wx_r, wc_s, wc_r, xs_s, xs_r, ar_s, ar_r, rs_s, rs_r, ag_s, ag_r, xf_s, xf_r,
 ):
     dp = lax.axis_index("dp")
     x = lax.axis_index("seq")
@@ -316,9 +316,14 @@
     drows[0:slots, :] = drecv[...]
     part_s[...] += lax.dot_general(
         drows[0:slots, :], weighted_s[0:slots, :], ROWS_T, preferred_element_type=jnp.float32)
-    c_send[...] = part_s[pl.ds(pl.multiple_of(oc * hc, 8), hc), :].astype(jnp.bfloat16)
-    c_copy = remote(c_send, c_recv, ar_s.at[0], ar_r.at[0], cdev)
+    given = part_s[pl.ds(pl.multiple_of(oc * hc, 8), hc), :]
+    left, right = given[:, 0:hc], given[:, hc:]
+    c_send[0] = jnp.where(first, right, left).astype(jnp.bfloat16)
+    c_copy = remote(c_send.at[0], c_recv.at[0], ar_s.at[0], ar_r.at[0], cdev)
     c_copy.start()
+    c_send[1] = jnp.where(first, left, right).astype(jnp.bfloat16)
+    c_copy2 = remote(c_send.at[1], c_recv.at[1], ar_s.at[2], ar_r.at[2], cdev)
+    c_copy2.start()
     pass_z(0)
     zbuf[3 * slots : 4 * slots, :] = lax.dot_general(
         weighted_s[slots:, :], p_ref[...], COLS_T, preferred_element_type=jnp.float32
@@ -330,12 +335,14 @@
     pass_y(0)
 
     c_copy.wait_recv()
-    half = part_s[pl.ds(pl.multiple_of(c * hc, 8), hc), :] + c_recv[...].astype(jnp.float32)
+    half = part_s[pl.ds(pl.multiple_of(c * hc, 8), hc), :]
     left, right = half[:, 0:hc], half[:, hc:]
-    x_send[...] = jnp.where(first, right, left).astype(jnp.bfloat16)
+    x_send[...] = (
+        jnp.where(first, right, left) + c_recv[0].astype(jnp.float32)).astype(jnp.bfloat16)
     x_copy = remote(x_send, x_recv, ar_s.at[1], ar_r.at[1], xdev)
     x_copy.start()
-    own_s[...] = jnp.where(first, left, right)
+    c_copy2.wait_recv()
+    own_s[...] = jnp.where(first, left, right) + c_recv[1].astype(jnp.float32)
 
     values = pre_ref[0].astype(jnp.float32)
     density = jnp.exp(-0.5 * values * values) / math.sqrt(2.0 * math.pi)
@@ -402,20 +409,26 @@
         cp.start()
         ag.append(cp)
 
+    xf = [remote(r_done.at[0:piece, :], fblock(c, x, me8 * piece, piece),
+                 xf_s.at[0], xf_r.at[0], xdev)]
+    xf[0].start()
+    for k in range(1, 8):
+        ag[k - 1].wait_recv()
+        block = fblock(c, x, lax.rem(me8 + 8 - k, 8) * piece, piece)
+        cp = remote(block, block, xf_s.at[k], xf_r.at[k], xdev)
+        cp.start()
+        xf.append(cp)
+    mine_to.wait()
+    quarter = fblock(c, x, 0, hc)
+    cq = remote(quarter, quarter, ar_s.at[3], ar_r.at[3], cdev)
+    cq.start()
     pass_x(1)
     pass_y(2)
-    mine_to.wait()
-    for cp in ag:
-        cp.wait_recv()
-    quarter = fblock(c, x, 0, hc)
-    xq = remote(quarter, quarter, ar_s.at[2], ar_r.at[2], xdev)
-    xq.start()
-    cq = remote(quarter, quarter, ar_s.at[3], ar_r.at[3], cdev)
-    cq.start()
     pass_x(2)
     pass_y(3)
     pass_x(3)
-    xq.wait_recv()
+    for cp in xf:
+        cp.wait_recv()
     other = fblock(c, ox, 0, hc)
     cq2 = remote(other, other, ar_s.at[4], ar_r.at[4], cdev)
     cq2.start()
@@ -452,7 +465,7 @@
             @pl.when(leaves)
             def _(d=d, s=s):
                 z_copy(d, s).wait_send()
-    for cp in [trunk_copy, d_copy, t_copy, h_copy, c_copy, x_copy, xq, cq, cq2] + ag:
+    for cp in [trunk_copy, d_copy, t_copy, h_copy, c_copy, c_copy2, x_copy, cq, cq2] + ag + xf:
         cp.wait_send()
 
 
@@ -472,10 +485,10 @@
         V((slots, chan), bf), V((slots, chan), bf), V((2 * slots, chan), bf),
         V((2 * slots, chan), bf), V((4 * slots + slab // 2, chan), bf),
         V((slab + 16, chan), f32), V((8, chan), f32), V((8, chan), f32),
-        V((chan, chan), f32), V((hc, chan), bf), V((hc, chan), bf), V((hc, hc), bf), V((hc, hc), bf),
+        V((chan, chan), f32), V((2, hc, hc), bf), V((2, hc, hc), bf), V((hc, hc), bf), V((hc, hc), bf),
         V((hc, hc), f32), V((hc, hc), bf), V((7, hc // 8, hc), bf), V((chan, chan), bf),
         D((6,)), D((6,)), D((7,)), D((7,)), D((7,)), D((7,)), D((21,)), D((21,)), D((4,)), D((4,)),
-        D((6,)), D((6,)), D((7,)), D((7,)), D((7,)), D((7,)),
+        D((6,)), D((6,)), D((7,)), D((7,)), D((7,)), D((7,)), D((8,)), D((8,)),
     ]
     return pl.pallas_call(
         kernel,

time: 59 us -> 61.6 us (1.044); the launches traced: 58.9 us -> 60.8 us
  Pallas kernels: 56.1 us -> 58 us
    pallas_call x1, Pallas kernels: 56.1 us -> 58 us  [per_device_kernel(): pl.pallas_call(kernel, out_shape=(jax.ShapeDtypeStruct(pre_act.shape, bf)...]
where the time goes in v4:
time: 61.6 us; the launch traced here: 60.8 us
  Pallas kernels  58 us (94%)
  local copies, waits for them, and re-layouts  2.15 us (3%)
  between operations  0.64 us (1%)
    pallas_call x1, Pallas kernels, per_device_kernel(): pl.pallas_call(kernel, out_shape=(jax.ShapeDtypeStruct(pre_act.shape, bf)...  58 us
    unnamed x2, local copies, waits for them, and re-layouts  2.15 us

profile of v4, /device:TPU:1, one launch (start us, length us, event | category | flops | bytes accessed | tf_op | source)
XLA Modules:
  0.0 60.8 jit_solution(11877617660935537440)
XLA Ops:
  0.6 58.0 %shard_map.95 = (bf16[1,256,768]{2,1,0:T(8,128)(2,1)S(1)}, f32[768,768]{1,0:T(8,128)S(1)}) custom-call(bf16[1,256,768]{2,1,0:T(8,128)(2,1)} %pre_hbm.1, bf16[1,256,384]{2,1,0:T(8,128)(2,1)} %trunk_ref.1, bf16[5,48,768]{2,1,0:T(8,128)(2,1)} %w_ref.1, bf16[768,768]{1,0:T(8,128)(2,1)} %p_hbm.1, s32[1,1,2,128]{3,2,1,0:T(2,128)} %ds_hbm.1, ...), custom_call_target="tpu_custom_call" | custom-call | tf_op jit(solution)/shard_map/pallas_call | solution.py:493
  58.6 0.7 %copy.12 = bf16[1,256,768]{2,1,0:T(8,128)(2,1)} copy(bf16[1,256,768]{2,1,0:T(8,128)(2,1)S(1)} %get-tuple-element.4) | data formatting | bytes 786432
  59.3 1.4 %copy.13 = f32[768,768]{1,0:T(8,128)} copy(f32[768,768]{1,0:T(8,128)S(1)} %get-tuple-element.5) | data formatting | bytes 4718592

commit v5 on v4

--- a/solution.py
+++ b/solution.py
@@ -409,6 +409,8 @@
         cp.start()
         ag.append(cp)
 
+    pass_x(1)
+    pass_y(2)
     xf = [remote(r_done.at[0:piece, :], fblock(c, x, me8 * piece, piece),
                  xf_s.at[0], xf_r.at[0], xdev)]
     xf[0].start()
@@ -422,8 +424,6 @@
     quarter = fblock(c, x, 0, hc)
     cq = remote(quarter, quarter, ar_s.at[3], ar_r.at[3], cdev)
     cq.start()
-    pass_x(1)
-    pass_y(2)
     pass_x(2)
     pass_y(3)
     pass_x(3)

time: 61.6 us -> 57.9 us (0.940)
  Pallas kernels: 58 us -> 54.2 us
    pallas_call x1, Pallas kernels: 58 us -> 54.2 us  [per_device_kernel(): pl.pallas_call(kernel, out_shape=(jax.ShapeDtypeStruct(pre_act.shape, bf)...]
where the time goes in v5:
time: 57.9 us; the launch traced here: 57 us
  Pallas kernels  54.2 us (94%)
  local copies, waits for them, and re-layouts  2.15 us (4%)
  between operations  0.64 us (1%)
    pallas_call x1, Pallas kernels, per_device_kernel(): pl.pallas_call(kernel, out_shape=(jax.ShapeDtypeStruct(pre_act.shape, bf)...  54.2 us
    unnamed x2, local copies, waits for them, and re-layouts  2.15 us

profile of v5, /device:TPU:1, one launch (start us, length us, event | category | flops | bytes accessed | tf_op | source)
XLA Modules:
  0.0 57.0 jit_solution(18434245592639460294)
XLA Ops:
  0.6 54.2 %shard_map.95 = (bf16[1,256,768]{2,1,0:T(8,128)(2,1)S(1)}, f32[768,768]{1,0:T(8,128)S(1)}) custom-call(bf16[1,256,768]{2,1,0:T(8,128)(2,1)} %pre_hbm.1, bf16[1,256,384]{2,1,0:T(8,128)(2,1)} %trunk_ref.1, bf16[5,48,768]{2,1,0:T(8,128)(2,1)} %w_ref.1, bf16[768,768]{1,0:T(8,128)(2,1)} %p_hbm.1, s32[1,1,2,128]{3,2,1,0:T(2,128)} %ds_hbm.1, ...), custom_call_target="tpu_custom_call" | custom-call | tf_op jit(solution)/shard_map/pallas_call | solution.py:493
  54.9 0.7 %copy.12 = bf16[1,256,768]{2,1,0:T(8,128)(2,1)} copy(bf16[1,256,768]{2,1,0:T(8,128)(2,1)S(1)} %get-tuple-element.4) | data formatting | bytes 786432
  55.6 1.4 %copy.13 = f32[768,768]{1,0:T(8,128)} copy(f32[768,768]{1,0:T(8,128)S(1)} %get-tuple-element.5) | data formatting | bytes 4718592
